TPU v7x, 256 devices: a whole 4x4x8 slice. The times are simulated.
256 devices in a mesh: win: 32 (over z, y_lo, core), chan: 8 (over x, y_hi).
Axes of the slice: x: 4, y: 4 (y_hi: 2, y_lo: 2; y = y_hi * 2 + y_lo), z: 8, core: 2. Of those that a mesh axis runs over, the one named last changes fastest.
Arguments:
- traces: bfloat16 [256, 1024, 4096], P('win', 'chan'), may hold values from -6 to 6
- source_block: int32 [3], replicated, may hold values from 0 to 7, as said below
- pair_source: int32 [3, 4096], P(None, 'chan'), may hold values from 0 to 127
- pair_receiver: int32 [3, 4096], P(None, 'chan'), may hold values from 0 to 127
- pair_bin: int32 [3, 4096], P(None, 'chan'), may hold values from 0 to 1023, as said below
- bin_slot: int32 [1024], replicated, may hold values from 0 to 1023, as said below
Outputs:
- stacks: float32 [3, 4096, 1024], P(None, 'win', 'chan')
Inputs may be any that keep to these rules, and one draw needn't show every extreme that they name: `source_block`: not every step names the same block; some step names block 0 and some step block 8 - 1. `pair_bin`: among the 512 pairs of one index of chan in a step, at most 128 have bins with bin_slot // 128 equal to one owner; in every step one owner gets exactly 128 from every index of chan. `bin_slot`: each bin has its own row.
All inputs are finite; a program needn't handle non-finite values.
Results may differ from a plain program's by a relative error of at most 0.0056.
Values may be sent and summed in bfloat16 or wider, within the bound.
No kernel may reach another device: no remote copies, remote signals or barrier semaphores. Data moves between devices by JAX's collectives and lax.ppermute only.
A program may use at most 64 MiB of HBM per device.

v0:
```python
import math
import jax
import jax.numpy as jnp
from jax import lax
from jax.sharding import PartitionSpec as P

WLEN = 4096
F = 128
FREQ0 = 256
LAGS = 4096
BIN_DEV = 128
STEPS = 3
P_DEV = 512


def from_root(block, axis, holder):
    block = jnp.where(lax.axis_index(axis) == holder, block, jnp.zeros_like(block))
    return lax.psum(block, axis)


def forward_table():
    samples = jnp.arange(WLEN, dtype=jnp.int32)
    freq_ids = FREQ0 + jnp.arange(F, dtype=jnp.int32)
    phases = samples[:, None] * freq_ids[None, :] % WLEN
    angles = phases.astype(jnp.float32) * (2.0 * math.pi / WLEN)
    return jnp.concatenate([jnp.cos(angles), -jnp.sin(angles)], axis=1).astype(jnp.bfloat16)


def lag_table(length, norm_scale):
    samples = jnp.arange(length, dtype=jnp.int32)
    freq_ids = FREQ0 + jnp.arange(F, dtype=jnp.int32)
    phases = freq_ids[:, None] * (samples[None, :] + (WLEN - LAGS // 2)) % WLEN
    angles = phases.astype(jnp.float32) * (2.0 * math.pi / WLEN)
    return jnp.concatenate([jnp.cos(angles), -jnp.sin(angles)], axis=0) * norm_scale


def cross_spectra(src_spec, rec_spec):
    src_re, src_im = (src_spec[..., :F], src_spec[..., F:])
    rec_re, rec_im = (rec_spec[..., :F], rec_spec[..., F:])
    real_part = jnp.sum(src_re * rec_re + src_im * rec_im, axis=0)
    imag_part = jnp.sum(src_re * rec_im - src_im * rec_re, axis=0)
    return jnp.concatenate([real_part, imag_part], axis=-1)


def project_lags(lag_basis, binned):
    return lax.dot_general(
        lag_basis, binned, (((0,), (1,)), ((), ())), precision=lax.Precision.HIGHEST
    )


def pick_channels(block, picks):
    chooser = (picks[:, None] == jnp.arange(block.shape[1], dtype=jnp.int32)[None, :]).astype(
        jnp.bfloat16
    )
    return jnp.einsum("pc,wcf->wpf", chooser, block, preferred_element_type=jnp.float32)


def on_device(traces, source_block, pair_source, pair_receiver, pair_bin, bin_slot):
    win_local, chan_local, samples_count = traces.shape
    chan_count = lax.axis_size("chan")
    win_count = lax.axis_size("win")
    lag_count = LAGS // win_count
    norm_scale = 1.0 / math.sqrt(2.0 * F * win_count * win_local)
    capacity = min(2 * P_DEV // chan_count, 3 * P_DEV // 4)
    spectra = jnp.dot(
        traces.reshape(win_local * chan_local, samples_count),
        forward_table(),
        preferred_element_type=jnp.float32,
    )
    power = jnp.mean(spectra * spectra, axis=-1, keepdims=True)
    whitened = (
        (spectra * lax.rsqrt(power + 1e-06))
        .astype(jnp.bfloat16)
        .reshape(win_local, chan_local, 2 * F)
    )
    bin_range = jnp.arange(bin_slot.shape[0], dtype=jnp.int32)
    pair_range = jnp.arange(P_DEV, dtype=jnp.int32)
    lower_tri = (pair_range[None, :] <= pair_range[:, None]).astype(jnp.bfloat16)
    results = []
    for section_index in range(STEPS):
        source = from_root(whitened, "chan", source_block[section_index])
        src_spec = pick_channels(source, pair_source[section_index])
        rec_spec = pick_channels(whitened, pair_receiver[section_index])
        partial_value = cross_spectra(src_spec, rec_spec).astype(jnp.bfloat16)
        matches_bin = pair_bin[section_index][:, None] == bin_range[None, :]
        slot_ids = jnp.sum(jnp.where(matches_bin, bin_slot[None, :], 0), axis=1)
        owners = slot_ids // BIN_DEV
        row_in_owner = slot_ids % BIN_DEV
        matches = owners[:, None] == jnp.arange(chan_count, dtype=jnp.int32)[None, :]
        running = jnp.dot(
            lower_tri, matches.astype(jnp.bfloat16), preferred_element_type=jnp.float32
        ).astype(jnp.int32)
        position = jnp.sum(jnp.where(matches, running - 1, 0), axis=1)
        target = owners * capacity + position
        slot_range = jnp.arange(chan_count * capacity, dtype=jnp.int32)
        placed = slot_range[:, None] == target[None, :]
        outgoing = jnp.dot(
            placed.astype(jnp.bfloat16), partial_value, preferred_element_type=jnp.float32
        )
        outgoing = outgoing.astype(jnp.bfloat16).reshape(chan_count, capacity, 2 * F)
        labels = jnp.sum(jnp.where(placed, row_in_owner[None, :] + 1, 0), axis=1) - 1
        labels = labels.reshape(chan_count, capacity)
        incoming, received_rows = (
            lax.all_to_all(outgoing, "chan", split_axis=0, concat_axis=0, tiled=True),
            lax.all_to_all(labels, "chan", split_axis=0, concat_axis=0, tiled=True),
        )
        onehot = (
            received_rows.reshape(-1)[None, :] == jnp.arange(BIN_DEV, dtype=jnp.int32)[:, None]
        ).astype(jnp.bfloat16)
        binned = jnp.dot(onehot, incoming.reshape(-1, 2 * F), preferred_element_type=jnp.float32)
        stacked = lax.psum_scatter(
            project_lags(lag_table(lag_count * lax.axis_size("win"), norm_scale), binned),
            "win",
            scatter_dimension=0,
            tiled=True,
        )
        results.append(stacked)
    return jnp.stack(results)


def solution(mesh):
    placed = (P("win", "chan", None), P(), P(None, "chan"), P(None, "chan"), P(None, "chan"), P())
    return jax.shard_map(
        on_device, mesh=mesh, in_specs=placed, out_specs=P(None, "win", "chan"), check_vma=False
    )
```

profile of v0, /device:TPU:2, one launch (start us, length us, event | category | flops | bytes accessed | tf_op | source)
XLA Modules:
  0.0 528.6 jit_solution(2868573302361774314)
XLA Ops:
  6.5 8.6 %cosine_convert_fusion = (bf16[4096,128]{1,0:T(8,128)(2,1)S(1)}, bf16[4096,128]{1,0:T(8,128)(2,1)S(1)}) fusion(s32[128]{0:T(128)S(1)} %iota_add_fusion.1), kind=kLoop, calls=%fused_computation.45 | loop fusion | flops 8912896 | bytes 2097664 | tf_op jit(solution)/shard_map/convert.6
  15.1 5.8 %multiply_reduce_fusion = (f32[1024]{0:T(1024)S(1)}, f32[256,1024]{1,0:T(8,128)S(1)}) fusion(bf16[1024,4096]{1,0:T(8,128)(2,1)} %bitcast.102, bf16[4096,128]{1,0:T(8,128)(2,1)S(1)} %get-tuple-element.41, bf16[4096,128]{1,0:T(8,128)(2,1)S(1)} %get-tuple-element.40), kind=kOutput, calls=%fused_computation.76 | convolution fusion | flops 2152201216 | bytes 11538432 | tf_op jit(solution)/shard_map/dot_general | solution.py:65
  23.6 1.4 bitcast_select_fusion.2
  25.0 1.2 select_reduce_fusion.5
  27.4 7.5 %all-to-all-start = ((s32[8,1,128]{2,1,0:T(1,128)}), s32[8,1,128]{2,1,0:T(1,128)S(1)}, u32[]{:S(2)}, u32[]{:S(2)}) async-start(s32[8,1,128]{2,1,0:T(1,128)} %bitcast.1), calls=%async_computation | async-start | bytes 8192 | tf_op jit(solution)/shard_map/all_to_all | solution.py:105
  35.1 2.7 convolution_bitcast_fusion.4
  37.8 92.9 %all-reduce.3.cloned.1.call-done = (bf16[8,128,256]{1,2,0:T(8,128)(2,1)}, bf16[8,128,256]{1,2,0:T(8,128)(2,1)}, bf16[8,128,256]{1,2,0:T(8,128)(2,1)}) async-done(((bf16[8,128,256]{1,2,0:T(8,128)(2,1)}, bf16[8,128,256]{1,2,0:T(8,128)(2,1)}, bf16[8,128,256]{1,2,0:T(8,128)(2,1)}), (bf16[8,128,256]{1,2,0:T(8,128)(2,1)}, bf16[8,128,256]{1,2,0:T(8,128)(2,1)}, ...) | async-done | bytes 1572880 | tf_op jit(solution)/shard_map/psum | solution.py:18
  130.7 2.0 convolution_bitcast_fusion.5
  134.2 1.3 fusion.22
  135.5 5.5 %all-to-all-start.1 = ((bf16[8,128,256]{2,1,0:T(8,128)(2,1)}), bf16[8,128,256]{2,1,0:T(8,128)(2,1)S(1)}, u32[]{:S(2)}, u32[]{:S(2)}) async-start(bf16[8,128,256]{2,1,0:T(8,128)(2,1)} %bitcast.12), calls=%async_computation.1 | async-start | bytes 1048576 | tf_op jit(solution)/shard_map/all_to_all | solution.py:104
  141.5 9.4 %fusion.37 = (f32[128,4096]{1,0:T(8,128)S(1)}, f32[128,4096]{1,0:T(8,128)}) fusion(s32[4096]{0:T(1024)S(1)} %iota_add_fusion, s32[128]{0:T(128)S(1)} %iota_add_fusion.1), kind=kLoop, calls=%fused_computation.79 | loop fusion | flops 7864320 | bytes 4211200 | tf_op jit(solution)/shard_map/cos | solution.py:34
  151.1 9.6 %fusion.2 = f32[4096,128]{1,0:T(8,128)} fusion(f32[128,256]{1,0:T(8,128)S(1)} %fusion.42, f32[128,4096]{1,0:T(8,128)} %get-tuple-element.21, f32[128,4096]{1,0:T(8,128)S(1)} %get-tuple-element.20), kind=kOutput, calls=%fused_computation.11 | convolution fusion | flops 1612709888 | bytes 6422528 | tf_op jit(solution)/shard_map/dot_general | solution.py:46
  161.9 7.2 %all-to-all-start.2 = ((s32[8,1,128]{2,1,0:T(1,128)}), s32[8,1,128]{2,1,0:T(1,128)S(1)}, u32[]{:S(2)}, u32[]{:S(2)}) async-start(s32[8,1,128]{2,1,0:T(1,128)} %bitcast.16), calls=%async_computation.3 | async-start | bytes 8192 | tf_op jit(solution)/shard_map/all_to_all | solution.py:105
  172.8 2.5 all-to-all-done.2
  175.2 13.2 %all_to_all.33 = bf16[8,128,256]{2,1,0:T(8,128)(2,1)S(1)} all-to-all(bf16[8,128,256]{2,1,0:T(8,128)(2,1)S(1)} %bitcast.85), channel_id=1, replica_groups=mesh['win'=32,'chan'=8] {'chan'}, dimensions={0} | all-to-all | bytes 1048576 | tf_op jit(solution)/shard_map/all_to_all | solution.py:104
  188.7 9.6 %fusion.1 = f32[4096,128]{1,0:T(8,128)} fusion(f32[128,256]{1,0:T(8,128)S(1)} %fusion.43, f32[128,4096]{1,0:T(8,128)} %get-tuple-element.21, f32[128,4096]{1,0:T(8,128)S(1)} %get-tuple-element.20), kind=kOutput, calls=%fused_computation.10 | convolution fusion | flops 1612709888 | bytes 6422528 | tf_op jit(solution)/shard_map/dot_general | solution.py:46
  199.6 4.8 all-to-all-start.4
  208.0 2.4 all-to-all-done.4
  210.5 12.6 %all_to_all.34 = bf16[8,128,256]{2,1,0:T(8,128)(2,1)S(1)} all-to-all(bf16[8,128,256]{2,1,0:T(8,128)(2,1)S(1)} %bitcast.86), channel_id=1, replica_groups=mesh['win'=32,'chan'=8] {'chan'}, dimensions={0} | all-to-all | bytes 1048576 | tf_op jit(solution)/shard_map/all_to_all | solution.py:104
  223.3 9.6 %fusion = f32[4096,128]{1,0:T(8,128)} fusion(f32[128,256]{1,0:T(8,128)S(1)} %fusion.44, f32[128,4096]{1,0:T(8,128)} %get-tuple-element.21, f32[128,4096]{1,0:T(8,128)S(1)} %get-tuple-element.20), kind=kOutput, calls=%fused_computation.9 | convolution fusion | flops 1612709888 | bytes 6422528 | tf_op jit(solution)/shard_map/dot_general | solution.py:46
  233.0 48.9 %reduce-scatter.4.cloned.1.call-done = f32[128,128]{1,0:T(8,128)} async-done(((f32[4096,128]{1,0:T(8,128)}), f32[128,128]{1,0:T(8,128)}) %reduce-scatter.4.cloned.1.call-update) | async-done | bytes 65552 | tf_op jit(solution)/shard_map/reduce_scatter | solution.py:111
  281.9 119.5 %reduce-scatter.6.cloned.1.call-done = f32[128,128]{1,0:T(8,128)} async-done(((f32[4096,128]{1,0:T(8,128)}), f32[128,128]{1,0:T(8,128)}) %reduce-scatter.6.cloned.1.call-update) | async-done | bytes 65552 | tf_op jit(solution)/shard_map/reduce_scatter | solution.py:111
  401.4 118.8 %reduce-scatter.8.cloned.1.call-done = f32[128,128]{1,0:T(8,128)} async-done(((f32[4096,128]{1,0:T(8,128)}), f32[128,128]{1,0:T(8,128)}) %reduce-scatter.8.cloned.1.call-update) | async-done | bytes 65552 | tf_op jit(solution)/shard_map/reduce_scatter | solution.py:111
  520.2 1.6 pad_maximum_fusion
  (60 shorter events, 14.3 us)
Async XLA Ops:
  6.5 124.2 %all-reduce.3.cloned.1.call-start = ((), (), s32[]{:S(2)}) async-start(), calls=%async_computation.12 | async-start | bytes 3145728 | tf_op jit(solution)/shard_map/psum | solution.py:18
  15.1 5.8 %copy-start.6 = (s32[3]{0:T(128)S(1)}, s32[3]{0:T(128)}, u32[]{:S(2)}) copy-start(s32[3]{0:T(128)} %param.7) | copy-start | bytes 40
  23.5 1.5 copy-start.3
  23.5 1.5 copy-start.7
  23.5 11.3 %copy-start.4 = (s32[3,512]{1,0:T(4,128)S(1)}, s32[3,512]{1,0:T(4,128)}, u32[]{:S(2)}) copy-start(s32[3,512]{1,0:T(4,128)} %param.8) | copy-start | bytes 18436
  23.6 11.3 %copy-start.5 = (s32[3,512]{1,0:T(4,128)S(1)}, s32[3,512]{1,0:T(4,128)}, u32[]{:S(2)}) copy-start(s32[3,512]{1,0:T(4,128)} %param.9) | copy-start | bytes 18436
  27.4 108.1 %all-to-all-start = ((s32[8,1,128]{2,1,0:T(1,128)}), s32[8,1,128]{2,1,0:T(1,128)S(1)}, u32[]{:S(2)}, u32[]{:S(2)}) async-start(s32[8,1,128]{2,1,0:T(1,128)} %bitcast.1), calls=%async_computation | async-start | bytes 8192 | tf_op jit(solution)/shard_map/all_to_all | solution.py:105
  130.7 2.3 copy-start
  135.5 15.4 %all-to-all-start.1 = ((bf16[8,128,256]{2,1,0:T(8,128)(2,1)}), bf16[8,128,256]{2,1,0:T(8,128)(2,1)S(1)}, u32[]{:S(2)}, u32[]{:S(2)}) async-start(bf16[8,128,256]{2,1,0:T(8,128)(2,1)} %bitcast.12), calls=%async_computation.1 | async-start | bytes 1048576 | tf_op jit(solution)/shard_map/all_to_all | solution.py:104
  141.0 140.8 %reduce-scatter.4.cloned.1.call-start = ((), (), s32[]{:S(2)}) async-start(), calls=%async_computation.9 | async-start | bytes 2162688 | tf_op jit(solution)/shard_map/reduce_scatter | solution.py:111
  161.9 13.3 %all-to-all-start.2 = ((s32[8,1,128]{2,1,0:T(1,128)}), s32[8,1,128]{2,1,0:T(1,128)S(1)}, u32[]{:S(2)}, u32[]{:S(2)}) async-start(s32[8,1,128]{2,1,0:T(1,128)} %bitcast.16), calls=%async_computation.3 | async-start | bytes 8192 | tf_op jit(solution)/shard_map/all_to_all | solution.py:105
  169.1 232.2 %reduce-scatter.6.cloned.1.call-start = ((), (), s32[]{:S(2)}) async-start(), calls=%async_computation.10 | async-start | bytes 2162688 | tf_op jit(solution)/shard_map/reduce_scatter | solution.py:111
  169.3 1.0 copy-start.2
  199.6 10.9 %all-to-all-start.4 = ((s32[8,1,128]{2,1,0:T(1,128)}), s32[8,1,128]{2,1,0:T(1,128)S(1)}, u32[]{:S(2)}, u32[]{:S(2)}) async-start(s32[8,1,128]{2,1,0:T(1,128)} %bitcast.29), calls=%async_computation.6 | async-start | bytes 8192 | tf_op jit(solution)/shard_map/all_to_all | solution.py:105
  204.3 315.9 %reduce-scatter.8.cloned.1.call-start = ((), (), s32[]{:S(2)}) async-start(), calls=%async_computation.11 | async-start | bytes 2162688 | tf_op jit(solution)/shard_map/reduce_scatter | solution.py:111
  204.6 1.0 copy-start.1
Sparse Core Ops, SparseCore 0:
  25.1 105.5 all-reduce.2
  160.9 120.9 reduce-scatter.3
  284.6 116.7 reduce-scatter.5
  403.7 116.4 reduce-scatter.7
where the time goes:
time: 536 us; the launch traced here: 529 us
  waiting for transfers between devices  385 us (72%)
  matrix products  46.4 us (9%)
  other arithmetic  28.2 us (5%)
  starting transfers between devices  25.9 us (5%)
  blocking collectives  25.9 us (5%)
  between operations  15.5 us (3%)
    reduce_scatter x3, waiting for transfers between devices, on_device(): lax.psum_scatter(project_lags(lag_table(lag_count * lax.axis_size('win'),...  287 us
    psum x1, waiting for transfers between devices, from_root(): return lax.psum(block, axis)  92.9 us
    dot_general x3, matrix products, project_lags(): lax.dot_general(lag_basis, binned, (((0,), (1,)), ((), ())), precision=la...  28.8 us
    all_to_all x2, blocking collectives, on_device(): lax.all_to_all(outgoing, 'chan', split_axis=0, concat_axis=0, tiled=True)  25.9 us
    all_to_all x3, starting transfers between devices, on_device(): lax.all_to_all(labels, 'chan', split_axis=0, concat_axis=0, tiled=True)  19.5 us
  transfers between devices with their start and end apart: 8, of which 6 were waited for; matrix products, arithmetic and copies ran while one was open for 9% of the time, Pallas kernels for 0%

commit v1 on v0

--- a/solution.py
+++ b/solution.py
@@ -15,7 +15,7 @@
 
 def from_root(block, axis, holder):
     block = jnp.where(lax.axis_index(axis) == holder, block, jnp.zeros_like(block))
-    return lax.psum(block, axis)
+    return jnp.sum(lax.all_gather(block, axis), axis=0)
 
 
 def forward_table():

time: 536 us -> 635 us (1.18)
  waiting for transfers between devices: 385 us -> 464 us
  other arithmetic: 28.2 us -> 35.9 us
    all_gather x0 -> x3, waiting for transfers between devices: none -> 134 us  [from_root(): return jnp.sum(lax.all_gather(block, axis), axis=0)]
    psum x1 -> x0, waiting for transfers between devices: 92.9 us -> none  [from_root(): return lax.psum(block, axis)]
    reduce_scatter x3, waiting for transfers between devices: 287 us -> 328 us  [on_device(): lax.psum_scatter(project_lags(lag_table(lag_count * lax.axis_size('win'),...]
    reduce_sum x0 -> x3, other arithmetic: none -> 8.9 us  [from_root(): return jnp.sum(lax.all_gather(block, axis), axis=0)]
  transfers between devices with their start and end apart: 8 -> 10, of which waited for: 6 -> 7; matrix products, arithmetic and copies ran while one was open for 9% -> 11% of each run, Pallas kernels for 0% -> 0%
where the time goes in v1:
time: 635 us; the launch traced here: 627 us
  waiting for transfers between devices  464 us (73%)
  matrix products  49.3 us (8%)
  other arithmetic  35.9 us (6%)
  blocking collectives  28.3 us (4%)
  starting transfers between devices  26.2 us (4%)
  between operations  16 us (3%)
  local copies, waits for them, and re-layouts  7.75 us (1%)
    reduce_scatter x3, waiting for transfers between devices, on_device(): lax.psum_scatter(project_lags(lag_table(lag_count * lax.axis_size('win'),...  328 us
    all_gather x3, waiting for transfers between devices, from_root(): return jnp.sum(lax.all_gather(block, axis), axis=0)  134 us
    dot_general x3, matrix products, project_lags(): lax.dot_general(lag_basis, binned, (((0,), (1,)), ((), ())), precision=la...  28.9 us
    all_to_all x2, blocking collectives, on_device(): lax.all_to_all(outgoing, 'chan', split_axis=0, concat_axis=0, tiled=True)  28.3 us
    all_to_all x3, starting transfers between devices, on_device(): lax.all_to_all(labels, 'chan', split_axis=0, concat_axis=0, tiled=True)  20.1 us
  transfers between devices with their start and end apart: 10, of which 7 were waited for; matrix products, arithmetic and copies ran while one was open for 11% of the time, Pallas kernels for 0%

profile of v1, /device:TPU:2, one launch (start us, length us, event | category | flops | bytes accessed | tf_op | source)
XLA Modules:
  0.0 627.0 jit_solution(4389534270755572728)
XLA Ops:
  6.5 8.6 %cosine_convert_fusion = (bf16[4096,128]{1,0:T(8,128)(2,1)S(1)}, bf16[4096,128]{1,0:T(8,128)(2,1)S(1)}) fusion(s32[128]{0:T(128)S(1)} %iota_add_fusion.1), kind=kLoop, calls=%fused_computation.45 | loop fusion | flops 8912896 | bytes 2097664 | tf_op jit(solution)/shard_map/convert.9
  15.1 5.8 multiply_reduce_fusion
  29.5 7.5 %all-to-all-start = ((s32[8,1,128]{2,1,0:T(1,128)}), s32[8,1,128]{2,1,0:T(1,128)S(1)}, u32[]{:S(2)}, u32[]{:S(2)}) async-start(s32[8,1,128]{2,1,0:T(1,128)} %bitcast.1), calls=%async_computation | async-start | bytes 8192 | tf_op jit(solution)/shard_map/all_to_all | solution.py:105
  37.0 2.8 convolution_bitcast_fusion.4
  39.8 62.3 %all-gather.4.cloned.1.call-done = bf16[8,8,128,256]{3,2,1,0:T(8,128)(2,1)} async-done(((bf16[1,8,128,256]{3,2,1,0:T(8,128)(2,1)}), bf16[8,8,128,256]{3,2,1,0:T(8,128)(2,1)}) %all-gather.4.cloned.1.call-update) | async-done | bytes 4194320 | tf_op jit(solution)/shard_map/all_gather | solution.py:18
  102.1 3.0 reduce_sum.184
  109.7 5.2 all-to-all-start.1
  115.3 9.4 %fusion.37 = (f32[128,4096]{1,0:T(8,128)S(1)}, f32[128,4096]{1,0:T(8,128)}) fusion(s32[4096]{0:T(1024)S(1)} %iota_add_fusion, s32[128]{0:T(128)S(1)} %iota_add_fusion.1), kind=kLoop, calls=%fused_computation.79 | loop fusion | flops 7864320 | bytes 4211200 | tf_op jit(solution)/shard_map/cos | solution.py:34
  126.5 9.6 %fusion.2 = f32[4096,128]{1,0:T(8,128)} fusion(f32[128,256]{1,0:T(8,128)S(1)} %fusion.41, f32[128,4096]{1,0:T(8,128)} %get-tuple-element.19, f32[128,4096]{1,0:T(8,128)S(1)} %get-tuple-element.18), kind=kOutput, calls=%fused_computation.11 | convolution fusion | flops 1612709888 | bytes 6422528 | tf_op jit(solution)/shard_map/dot_general | solution.py:46
  137.3 6.5 %all-to-all-start.2 = ((s32[8,1,128]{2,1,0:T(1,128)}), s32[8,1,128]{2,1,0:T(1,128)S(1)}, u32[]{:S(2)}, u32[]{:S(2)}) async-start(s32[8,1,128]{2,1,0:T(1,128)} %bitcast.17), calls=%async_computation.3 | async-start | bytes 8192 | tf_op jit(solution)/shard_map/all_to_all | solution.py:105
  144.0 2.8 convolution_bitcast_fusion.2
  146.8 34.4 %all-gather.6.cloned.1.call-done = bf16[8,8,128,256]{3,2,1,0:T(8,128)(2,1)} async-done(((bf16[1,8,128,256]{3,2,1,0:T(8,128)(2,1)}), bf16[8,8,128,256]{3,2,1,0:T(8,128)(2,1)}) %all-gather.6.cloned.1.call-update) | async-done | bytes 4194320 | tf_op jit(solution)/shard_map/all_gather | solution.py:18
  181.2 3.0 reduce_sum.190
  188.0 14.0 %all_to_all.33 = bf16[8,128,256]{2,1,0:T(8,128)(2,1)S(1)} all-to-all(bf16[8,128,256]{2,1,0:T(8,128)(2,1)S(1)} %bitcast.98), channel_id=1, replica_groups=mesh['win'=32,'chan'=8] {'chan'}, dimensions={0} | all-to-all | bytes 1048576 | tf_op jit(solution)/shard_map/all_to_all | solution.py:104
  202.2 9.7 %fusion.1 = f32[4096,128]{1,0:T(8,128)} fusion(f32[128,256]{1,0:T(8,128)S(1)} %fusion.42, f32[128,4096]{1,0:T(8,128)} %get-tuple-element.19, f32[128,4096]{1,0:T(8,128)S(1)} %get-tuple-element.18), kind=kOutput, calls=%fused_computation.10 | convolution fusion | flops 1612709888 | bytes 6422528 | tf_op jit(solution)/shard_map/dot_general | solution.py:46
  213.1 6.1 all-to-all-start.4
  219.5 2.8 convolution_bitcast_fusion
  222.3 37.0 %all-gather.8.cloned.1.call-done = bf16[8,8,128,256]{3,2,1,0:T(8,128)(2,1)} async-done(((bf16[1,8,128,256]{3,2,1,0:T(8,128)(2,1)}), bf16[8,8,128,256]{3,2,1,0:T(8,128)(2,1)}) %all-gather.8.cloned.1.call-update) | async-done | bytes 4194320 | tf_op jit(solution)/shard_map/all_gather | solution.py:18
  259.3 3.0 reduce_sum.196
  266.0 14.4 %all_to_all.34 = bf16[8,128,256]{2,1,0:T(8,128)(2,1)S(1)} all-to-all(bf16[8,128,256]{2,1,0:T(8,128)(2,1)S(1)} %bitcast.99), channel_id=1, replica_groups=mesh['win'=32,'chan'=8] {'chan'}, dimensions={0} | all-to-all | bytes 1048576 | tf_op jit(solution)/shard_map/all_to_all | solution.py:104
  280.6 9.6 %fusion = f32[4096,128]{1,0:T(8,128)} fusion(f32[128,256]{1,0:T(8,128)S(1)} %fusion.43, f32[128,4096]{1,0:T(8,128)} %get-tuple-element.19, f32[128,4096]{1,0:T(8,128)S(1)} %get-tuple-element.18), kind=kOutput, calls=%fused_computation.9 | convolution fusion | flops 1612709888 | bytes 6422528 | tf_op jit(solution)/shard_map/dot_general | solution.py:46
  290.2 89.3 %reduce-scatter.4.cloned.1.call-done = f32[128,128]{1,0:T(8,128)} async-done(((f32[4096,128]{1,0:T(8,128)}), f32[128,128]{1,0:T(8,128)}) %reduce-scatter.4.cloned.1.call-update) | async-done | bytes 65552 | tf_op jit(solution)/shard_map/reduce_scatter | solution.py:111
  379.6 119.5 %reduce-scatter.6.cloned.1.call-done = f32[128,128]{1,0:T(8,128)} async-done(((f32[4096,128]{1,0:T(8,128)}), f32[128,128]{1,0:T(8,128)}) %reduce-scatter.6.cloned.1.call-update) | async-done | bytes 65552 | tf_op jit(solution)/shard_map/reduce_scatter | solution.py:111
  499.1 119.3 %reduce-scatter.8.cloned.1.call-done = f32[128,128]{1,0:T(8,128)} async-done(((f32[4096,128]{1,0:T(8,128)}), f32[128,128]{1,0:T(8,128)}) %reduce-scatter.8.cloned.1.call-update) | async-done | bytes 65552 | tf_op jit(solution)/shard_map/reduce_scatter | solution.py:111
  (72 shorter events, 25.7 us)
Async XLA Ops:
  6.5 95.6 %all-gather.4.cloned.1.call-start = ((), (), s32[]{:S(2)}) async-start(), calls=%async_computation.9 | async-start | bytes 4718592 | tf_op jit(solution)/shard_map/all_gather | solution.py:18
  15.1 5.8 copy-start.6
  23.5 157.7 %all-gather.6.cloned.1.call-start = ((), (), s32[]{:S(2)}) async-start(), calls=%async_computation.11 | async-start | bytes 4718592 | tf_op jit(solution)/shard_map/all_gather | solution.py:18
  24.8 2.2 copy-start.3
  24.8 2.3 copy-start.7
  24.9 12.0 %copy-start.4 = (s32[3,512]{1,0:T(4,128)S(1)}, s32[3,512]{1,0:T(4,128)}, u32[]{:S(2)}) copy-start(s32[3,512]{1,0:T(4,128)} %param.9) | copy-start | bytes 18436
  24.9 12.0 %copy-start.5 = (s32[3,512]{1,0:T(4,128)S(1)}, s32[3,512]{1,0:T(4,128)}, u32[]{:S(2)}) copy-start(s32[3,512]{1,0:T(4,128)} %param.8) | copy-start | bytes 18436
  26.0 233.3 %all-gather.8.cloned.1.call-start = ((), (), s32[]{:S(2)}) async-start(), calls=%async_computation.13 | async-start | bytes 4718592 | tf_op jit(solution)/shard_map/all_gather | solution.py:18
  29.5 80.2 %all-to-all-start = ((s32[8,1,128]{2,1,0:T(1,128)}), s32[8,1,128]{2,1,0:T(1,128)S(1)}, u32[]{:S(2)}, u32[]{:S(2)}) async-start(s32[8,1,128]{2,1,0:T(1,128)} %bitcast.1), calls=%async_computation | async-start | bytes 8192 | tf_op jit(solution)/shard_map/all_to_all | solution.py:105
  105.1 2.2 copy-start.1
  109.7 16.6 %all-to-all-start.1 = ((bf16[8,128,256]{2,1,0:T(8,128)(2,1)}), bf16[8,128,256]{2,1,0:T(8,128)(2,1)S(1)}, u32[]{:S(2)}, u32[]{:S(2)}) async-start(bf16[8,128,256]{2,1,0:T(8,128)(2,1)} %bitcast.13), calls=%async_computation.1 | async-start | bytes 1048576 | tf_op jit(solution)/shard_map/all_to_all | solution.py:104
  114.8 264.7 %reduce-scatter.4.cloned.1.call-start = ((), (), s32[]{:S(2)}) async-start(), calls=%async_computation.10 | async-start | bytes 2162688 | tf_op jit(solution)/shard_map/reduce_scatter | solution.py:111
  137.3 50.7 %all-to-all-start.2 = ((s32[8,1,128]{2,1,0:T(1,128)}), s32[8,1,128]{2,1,0:T(1,128)S(1)}, u32[]{:S(2)}, u32[]{:S(2)}) async-start(s32[8,1,128]{2,1,0:T(1,128)} %bitcast.17), calls=%async_computation.3 | async-start | bytes 8192 | tf_op jit(solution)/shard_map/all_to_all | solution.py:105
  143.8 355.3 %reduce-scatter.6.cloned.1.call-start = ((), (), s32[]{:S(2)}) async-start(), calls=%async_computation.12 | async-start | bytes 2162688 | tf_op jit(solution)/shard_map/reduce_scatter | solution.py:111
  184.2 2.2 copy-start.2
  213.1 52.9 %all-to-all-start.4 = ((s32[8,1,128]{2,1,0:T(1,128)}), s32[8,1,128]{2,1,0:T(1,128)S(1)}, u32[]{:S(2)}, u32[]{:S(2)}) async-start(s32[8,1,128]{2,1,0:T(1,128)} %bitcast.31), calls=%async_computation.6 | async-start | bytes 8192 | tf_op jit(solution)/shard_map/all_to_all | solution.py:105
  219.3 399.1 %reduce-scatter.8.cloned.1.call-start = ((), (), s32[]{:S(2)}) async-start(), calls=%async_computation.14 | async-start | bytes 2162688 | tf_op jit(solution)/shard_map/reduce_scatter | solution.py:111
  262.2 2.2 copy-start
Sparse Core Ops, SparseCore 0:
  23.6 78.4 all-gather.3
  104.7 76.4 all-gather.5
  183.9 75.3 all-gather.7
  261.6 117.8 reduce-scatter.3
  382.1 116.9 reduce-scatter.5
  501.5 116.8 reduce-scatter.7
